TPU v7x, 128 devices: a whole 4x4x4 slice. The times are simulated.
128 devices in a mesh: tm: 2 (over z_hi), lon: 16 (over y, x), head: 4 (over z_lo, core).
Axes of the slice: x: 4, y: 4, z: 4 (z_hi: 2, z_lo: 2; z = z_hi * 2 + z_lo), core: 2. Of those that a mesh axis runs over, the one named last changes fastest.
Arguments:
- query_rows: bfloat16 [8, 8, 128, 5120], P('tm', None, 'lon', 'head'), may hold values from -16 to 16
- key_rows: bfloat16 [8, 8, 128, 5120], P('tm', None, 'lon', 'head'), may hold values from -16 to 16
- value_rows: bfloat16 [8, 8, 128, 5120], P('tm', None, 'lon', 'head'), may hold values from -6 to 6
- out_grad: bfloat16 [8, 8, 128, 5120], P('tm', None, 'lon', 'head'), may hold values from -6 to 6
- window_offsets: int32 [2, 2, 32], P('tm', None, 'lon'), may hold values from -1 to 1
Outputs:
- attended: bfloat16 [8, 8, 128, 5120], P('tm', None, 'lon', 'head')
- query_grad: bfloat16 [8, 8, 128, 5120], P('tm', None, 'lon', 'head')
- key_grad: bfloat16 [8, 8, 128, 5120], P('tm', None, 'lon', 'head')
- value_grad: bfloat16 [8, 8, 128, 5120], P('tm', None, 'lon', 'head')
All inputs are finite; a program needn't handle non-finite values.
Results may differ from a plain program's by a relative error of at most 0.013.
The roundings to bfloat16 on the way count: a program that leaves them out, or rounds other values in their place, can miss the bound.
Values may be sent and summed in bfloat16 or wider, within the bound.
A program may use at most 128 MiB of HBM per device.

v0:
```python
import math

import jax
import jax.numpy as jnp
from jax import lax
from jax.sharding import PartitionSpec as P

HD = 128
TILE = 4


def partner(block, axis, distance):
    count = lax.axis_size(axis)
    route = []
    for low in range(count):
        high = low | 1 << distance
        if high != low and high < count:
            route += [(low, high), (high, low)]
    return lax.ppermute(block, axis, route)


def extended(array, sides, width):
    for axis, dim in sides:
        count, length = (lax.axis_size(axis), array.shape[dim])
        up = [(i, (i + 1) % count) for i in range(count)]
        down = [(j, i) for i, j in up]
        last = lax.slice_in_dim(array, length - width, length, axis=dim)
        leading = lax.slice_in_dim(array, 0, width, axis=dim)
        before = lax.ppermute(last, axis, up)
        after = lax.ppermute(leading, axis, down)
        array = jnp.concatenate([before, array, after], axis=dim)
    return array


def passed_along(block, axis, distance):
    devices = range(lax.axis_size(axis))
    route = [((i - distance) % len(devices), i) for i in devices]
    return lax.ppermute(block, axis, route)


def widen_frames(stacked, frame_index):
    depth = stacked.shape[1]
    inward = partner(stacked, "tm", 0)
    joined = jnp.concatenate([inward, stacked, inward], axis=1)
    return lax.dynamic_slice_in_dim(joined, (1 - frame_index) * TILE, depth + TILE, 1)


def widen_lon(stacked):
    return extended(stacked, (("lon", 3),), 2 * TILE)


def return_lon(key_part, value_part):
    rim_cells = 2 * TILE
    low_rim = jnp.stack([key_part[:, :, :rim_cells], value_part[:, :, :rim_cells]])
    high_rim = jnp.stack([key_part[:, :, -rim_cells:], value_part[:, :, -rim_cells:]])
    from_next = passed_along(low_rim.astype(jnp.bfloat16), "lon", -1).astype(low_rim.dtype)
    from_prior = passed_along(high_rim.astype(jnp.bfloat16), "lon", 1).astype(high_rim.dtype)
    inner_key = key_part[:, :, rim_cells:-rim_cells]
    inner_value = value_part[:, :, rim_cells:-rim_cells]
    inner_key = (
        inner_key.at[:, :, -rim_cells:].add(from_next[0]).at[:, :, :rim_cells].add(from_prior[0])
    )
    inner_value = (
        inner_value.at[:, :, -rim_cells:].add(from_next[1]).at[:, :, :rim_cells].add(from_prior[1])
    )
    return (inner_key, inner_value)


def return_frames(key_part, value_part, frame_index):
    depth = key_part.shape[0] - TILE
    send_start = (1 - frame_index) * depth
    outward = jnp.stack(
        [
            lax.dynamic_slice_in_dim(key_part, send_start, TILE, 0),
            lax.dynamic_slice_in_dim(value_part, send_start, TILE, 0),
        ]
    )
    inward = partner(outward.astype(jnp.bfloat16), "tm", 0).astype(outward.dtype)
    own_start = frame_index * TILE
    own_key = lax.dynamic_slice_in_dim(key_part, own_start, depth, 0)
    own_value = lax.dynamic_slice_in_dim(value_part, own_start, depth, 0)
    own_key = own_key + inward[0]
    own_value = own_value + inward[1]
    return (own_key, own_value)


def window_rows(
    window_offsets, frame_index, frame_tiles, lat_tiles, lon_tiles, key_frames, lat_cells, key_lon
):
    group_shape = (frame_tiles, lat_tiles, lon_tiles)
    group_frame = jnp.broadcast_to(jnp.arange(frame_tiles)[:, None, None], group_shape).reshape(-1)
    group_lat = jnp.broadcast_to(jnp.arange(lat_tiles)[None, :, None], group_shape).reshape(-1)
    group_lon = jnp.broadcast_to(jnp.arange(lon_tiles)[None, None, :], group_shape).reshape(-1)
    group_shift = window_offsets.reshape(-1)
    frame_span = jnp.arange(key_frames)
    cell_span = jnp.arange(3 * TILE)
    lat_pos = jnp.clip(group_lat[:, None] * TILE - TILE + cell_span[None, :], 0, lat_cells - 1)
    lon_pos = (group_lon + group_shift + 1)[:, None] * TILE + cell_span[None, :]
    flat_index = (
        frame_span[None, :, None, None] * lat_cells + lat_pos[:, None, :, None]
    ) * key_lon + lon_pos[:, None, None, :]
    group_count = group_frame.shape[0]
    flat_index = flat_index.reshape(group_count, -1)
    key_tile = frame_span // TILE
    query_tile = frame_index * frame_tiles + group_frame
    frame_ok = jnp.abs(key_tile[None, :] - query_tile[:, None]) <= 1
    lat_step = group_lat[:, None] - 1 + cell_span[None, :] // TILE
    lat_ok = (lat_step >= 0) & (lat_step < lat_tiles)
    allowed = frame_ok[:, :, None, None] & lat_ok[:, None, :, None]
    allowed = jnp.broadcast_to(allowed, (group_count, key_frames, 3 * TILE, 3 * TILE)).reshape(
        group_count, -1
    )
    return (flat_index, allowed)


def on_device(query_rows, key_rows, value_rows, out_grad, window_offsets):
    frame_depth, lat_cells, lon_cells, width = query_rows.shape
    head_count = width // HD
    scale = 1.0 / math.sqrt(HD)
    frame_tiles = frame_depth // TILE
    lat_tiles = lat_cells // TILE
    lon_tiles = lon_cells // TILE
    group_count = frame_tiles * lat_tiles * lon_tiles
    frame_index = lax.axis_index("tm")
    stacked = jnp.stack([key_rows, value_rows])
    widened = widen_lon(widen_frames(stacked, frame_index))
    key_frames = widened.shape[1]
    key_lon = widened.shape[3]
    key_flat = widened[0].reshape(-1, width)
    value_flat = widened[1].reshape(-1, width)
    key_count = key_flat.shape[0]
    flat_index, allowed = window_rows(
        window_offsets,
        frame_index,
        frame_tiles,
        lat_tiles,
        lon_tiles,
        key_frames,
        lat_cells,
        key_lon,
    )
    allowed = allowed[:, None, :]
    tile_rows = TILE * TILE * TILE

    def to_groups(array):
        shaped = array.reshape(frame_tiles, TILE, lat_tiles, TILE, lon_tiles, TILE, width)
        return shaped.transpose(0, 2, 4, 1, 3, 5, 6).reshape(group_count, tile_rows, width)

    def from_groups(array):
        shaped = array.reshape(frame_tiles, lat_tiles, lon_tiles, TILE, TILE, TILE, width)
        return shaped.transpose(0, 3, 1, 4, 2, 5, 6).reshape(
            frame_depth, lat_cells, lon_cells, width
        )

    query_groups = to_groups(query_rows)
    grad_groups = to_groups(out_grad)
    index_rows = flat_index.reshape(-1)

    def one_head(head_index, carry):
        attended, query_grad, key_grad, value_grad = carry
        start = head_index * HD
        query_head = lax.dynamic_slice_in_dim(query_groups, start, HD, 2)
        grad_head = lax.dynamic_slice_in_dim(grad_groups, start, HD, 2)
        key_block = jnp.take(lax.dynamic_slice_in_dim(key_flat, start, HD, 1), flat_index, axis=0)
        value_block = jnp.take(
            lax.dynamic_slice_in_dim(value_flat, start, HD, 1), flat_index, axis=0
        )
        scores = (
            jnp.einsum("gqd,gkd->gqk", query_head, key_block, preferred_element_type=jnp.float32)
            * scale
        )
        peak = jnp.max(jnp.where(allowed, scores, -jnp.inf), axis=2, keepdims=True)
        expo = jnp.exp(jnp.where(allowed, scores - peak, -jnp.inf))
        probs = (expo / jnp.sum(expo, axis=2, keepdims=True)).astype(jnp.bfloat16)
        out_head = jnp.einsum(
            "gqk,gkd->gqd", probs, value_block, preferred_element_type=jnp.float32
        ).astype(jnp.bfloat16)
        delta = jnp.sum(
            grad_head.astype(jnp.float32) * out_head.astype(jnp.float32), axis=2, keepdims=True
        )
        dprobs = jnp.einsum(
            "gqd,gkd->gqk", grad_head, value_block, preferred_element_type=jnp.float32
        )
        dscores = (probs.astype(jnp.float32) * (dprobs - delta)).astype(jnp.bfloat16)
        query_head_grad = (
            jnp.einsum("gqk,gkd->gqd", dscores, key_block, preferred_element_type=jnp.float32)
            * scale
        ).astype(jnp.bfloat16)
        key_block_grad = (
            jnp.einsum("gqk,gqd->gkd", dscores, query_head, preferred_element_type=jnp.float32)
            * scale
        )
        value_block_grad = jnp.einsum(
            "gqk,gqd->gkd", probs, grad_head, preferred_element_type=jnp.float32
        )
        empty = jnp.zeros((key_count, HD), jnp.float32)
        key_head_grad = empty.at[index_rows].add(key_block_grad.reshape(-1, HD))
        value_head_grad = empty.at[index_rows].add(value_block_grad.reshape(-1, HD))
        attended = lax.dynamic_update_slice_in_dim(attended, out_head, start, 2)
        query_grad = lax.dynamic_update_slice_in_dim(query_grad, query_head_grad, start, 2)
        key_grad = lax.dynamic_update_slice_in_dim(key_grad, key_head_grad, start, 1)
        value_grad = lax.dynamic_update_slice_in_dim(value_grad, value_head_grad, start, 1)
        return (attended, query_grad, key_grad, value_grad)

    initial = (
        jnp.zeros((group_count, tile_rows, width), jnp.bfloat16),
        jnp.zeros((group_count, tile_rows, width), jnp.bfloat16),
        jnp.zeros((key_count, width), jnp.float32),
        jnp.zeros((key_count, width), jnp.float32),
    )
    attended, query_grad, key_grad, value_grad = lax.fori_loop(0, head_count, one_head, initial)
    grown_shape = (key_frames, lat_cells, key_lon, width)
    key_grad = key_grad.reshape(grown_shape)
    value_grad = value_grad.reshape(grown_shape)
    key_grad, value_grad = return_lon(key_grad, value_grad)
    key_grad, value_grad = return_frames(key_grad, value_grad, frame_index)
    return (
        from_groups(attended),
        from_groups(query_grad),
        key_grad.astype(jnp.bfloat16),
        value_grad.astype(jnp.bfloat16),
    )


def solution(mesh):
    in_specs = (
        P("tm", None, "lon", "head"),
        P("tm", None, "lon", "head"),
        P("tm", None, "lon", "head"),
        P("tm", None, "lon", "head"),
        P("tm", None, "lon"),
    )
    out_specs = (
        P("tm", None, "lon", "head"),
        P("tm", None, "lon", "head"),
        P("tm", None, "lon", "head"),
        P("tm", None, "lon", "head"),
    )
    return jax.shard_map(
        on_device, mesh=mesh, in_specs=in_specs, out_specs=out_specs, check_vma=False
    )
```

profile of v0, /device:TPU:0, one launch (start us, length us, event | category | flops | bytes accessed | tf_op | source)
XLA Modules:
  0.0 1107.6 jit_solution(5848175036981786646)
XLA Ops:
  6.2 28.9 %collective-permute-done = bf16[2,4,8,8,1280]{4,3,2,1,0:T(8,128)(2,1)} collective-permute-done((bf16[2,4,8,8,1280]{4,3,2,1,0:T(8,128)(2,1)S(1)}, bf16[2,4,8,8,1280]{4,3,2,1,0:T(8,128)(2,1)}, u32[]{:S(2)}, u32[]{:S(2)}) %collective-permute-start) | collective-permute-done | bytes 1310752 | tf_op jit(solution)/shard_map/ppermute | solution.py:19
  54.5 44.0 %collective-permute-done.2 = bf16[2,8,8,8,1280]{4,3,2,1,0:T(8,128)(2,1)} collective-permute-done((bf16[2,8,8,8,1280]{4,3,2,1,0:T(8,128)(2,1)S(1)}, bf16[2,8,8,8,1280]{4,3,2,1,0:T(8,128)(2,1)}, u32[]{:S(2)}, u32[]{:S(2)}) %collective-permute-start.2) | collective-permute-done | bytes 2621472 | tf_op jit(solution)/shard_map/ppermute | solution.py:30
  119.9 875.5 %while.29 = (s32[]{:T(128)}, bf16[4,64,1280]{2,1,0:T(8,128)(2,1)}, bf16[4,64,1280]{2,1,0:T(8,128)(2,1)}, f32[1536,1280]{1,0:T(8,128)}, f32[1536,1280]{1,0:T(8,12...) while((s32[]{:T(128)}, bf16[4,64,1280]{2,1,0:T(8,128)(2,1)}, ...), condition=%wide.region_6.8_spmd.clone.clone, body=%wide.region_0.7_spmd.clone.clone.sunk | while | flops 460652928 | bytes 37832076 | solution.py:211
  122.9 8.8 gather_fusion
  131.7 8.8 gather_fusion.1
  152.1 25.3 %scatter_custom_fusion.15 = f32[1536,128]{1,0:T(8,128)S(1)} fusion(s32[4608]{0:T(1024)S(1)} %fusion.91, f32[4608,128]{1,0:T(8,128)S(1)} %bitcast.93, f32[]{:T(128)} %constant.241.clone.1..sunk), kind=kCustom, calls=%fused_computation.33.clone.1 | custom fusion | flops 589824 | bytes 786436 | tf_op jit(solution)/shard_map/while/body/eval_jaxpr/scatter-add | solution.py:197
  180.5 25.6 %scatter_custom_fusion.14 = f32[1536,128]{1,0:T(8,128)S(1)} fusion(s32[4608]{0:T(1024)S(1)} %fusion.91, f32[4608,128]{1,0:T(8,128)} %bitcast.92, f32[]{:T(128)} %constant.241.clone.1..sunk), kind=kCustom, calls=%fused_computation.31.clone.1 | custom fusion | flops 589824 | bytes 786944 | tf_op jit(solution)/shard_map/while/body/eval_jaxpr/scatter-add | solution.py:198
  210.4 8.8 gather_fusion
  239.6 25.3 %scatter_custom_fusion.15 = f32[1536,128]{1,0:T(8,128)S(1)} fusion(s32[4608]{0:T(1024)S(1)} %fusion.91, f32[4608,128]{1,0:T(8,128)S(1)} %bitcast.93, f32[]{:T(128)} %constant.241.clone.1..sunk), kind=kCustom, calls=%fused_computation.33.clone.1 | custom fusion | flops 589824 | bytes 786436 | tf_op jit(solution)/shard_map/while/body/eval_jaxpr/scatter-add | solution.py:197
  268.0 25.6 %scatter_custom_fusion.14 = f32[1536,128]{1,0:T(8,128)S(1)} fusion(s32[4608]{0:T(1024)S(1)} %fusion.91, f32[4608,128]{1,0:T(8,128)} %bitcast.92, f32[]{:T(128)} %constant.241.clone.1..sunk), kind=kCustom, calls=%fused_computation.31.clone.1 | custom fusion | flops 589824 | bytes 786944 | tf_op jit(solution)/shard_map/while/body/eval_jaxpr/scatter-add | solution.py:198
  306.8 8.8 gather_fusion.1
  327.2 25.3 %scatter_custom_fusion.15 = f32[1536,128]{1,0:T(8,128)S(1)} fusion(s32[4608]{0:T(1024)S(1)} %fusion.91, f32[4608,128]{1,0:T(8,128)S(1)} %bitcast.93, f32[]{:T(128)} %constant.241.clone.1..sunk), kind=kCustom, calls=%fused_computation.33.clone.1 | custom fusion | flops 589824 | bytes 786436 | tf_op jit(solution)/shard_map/while/body/eval_jaxpr/scatter-add | solution.py:197
  355.6 25.6 %scatter_custom_fusion.14 = f32[1536,128]{1,0:T(8,128)S(1)} fusion(s32[4608]{0:T(1024)S(1)} %fusion.91, f32[4608,128]{1,0:T(8,128)} %bitcast.92, f32[]{:T(128)} %constant.241.clone.1..sunk), kind=kCustom, calls=%fused_computation.31.clone.1 | custom fusion | flops 589824 | bytes 786944 | tf_op jit(solution)/shard_map/while/body/eval_jaxpr/scatter-add | solution.py:198
  385.5 8.8 gather_fusion
  394.3 8.8 gather_fusion.1
  414.7 25.3 %scatter_custom_fusion.15 = f32[1536,128]{1,0:T(8,128)S(1)} fusion(s32[4608]{0:T(1024)S(1)} %fusion.91, f32[4608,128]{1,0:T(8,128)S(1)} %bitcast.93, f32[]{:T(128)} %constant.241.clone.1..sunk), kind=kCustom, calls=%fused_computation.33.clone.1 | custom fusion | flops 589824 | bytes 786436 | tf_op jit(solution)/shard_map/while/body/eval_jaxpr/scatter-add | solution.py:197
  443.1 25.6 %scatter_custom_fusion.14 = f32[1536,128]{1,0:T(8,128)S(1)} fusion(s32[4608]{0:T(1024)S(1)} %fusion.91, f32[4608,128]{1,0:T(8,128)} %bitcast.92, f32[]{:T(128)} %constant.241.clone.1..sunk), kind=kCustom, calls=%fused_computation.31.clone.1 | custom fusion | flops 589824 | bytes 786944 | tf_op jit(solution)/shard_map/while/body/eval_jaxpr/scatter-add | solution.py:198
  502.3 25.3 %scatter_custom_fusion.15 = f32[1536,128]{1,0:T(8,128)S(1)} fusion(s32[4608]{0:T(1024)S(1)} %fusion.91, f32[4608,128]{1,0:T(8,128)S(1)} %bitcast.93, f32[]{:T(128)} %constant.241.clone.1..sunk), kind=kCustom, calls=%fused_computation.33.clone.1 | custom fusion | flops 589824 | bytes 786436 | tf_op jit(solution)/shard_map/while/body/eval_jaxpr/scatter-add | solution.py:197
  530.7 25.6 %scatter_custom_fusion.14 = f32[1536,128]{1,0:T(8,128)S(1)} fusion(s32[4608]{0:T(1024)S(1)} %fusion.91, f32[4608,128]{1,0:T(8,128)} %bitcast.92, f32[]{:T(128)} %constant.241.clone.1..sunk), kind=kCustom, calls=%fused_computation.31.clone.1 | custom fusion | flops 589824 | bytes 786944 | tf_op jit(solution)/shard_map/while/body/eval_jaxpr/scatter-add | solution.py:198
  589.8 25.3 %scatter_custom_fusion.15 = f32[1536,128]{1,0:T(8,128)S(1)} fusion(s32[4608]{0:T(1024)S(1)} %fusion.91, f32[4608,128]{1,0:T(8,128)S(1)} %bitcast.93, f32[]{:T(128)} %constant.241.clone.1..sunk), kind=kCustom, calls=%fused_computation.33.clone.1 | custom fusion | flops 589824 | bytes 786436 | tf_op jit(solution)/shard_map/while/body/eval_jaxpr/scatter-add | solution.py:197
  618.2 25.6 %scatter_custom_fusion.14 = f32[1536,128]{1,0:T(8,128)S(1)} fusion(s32[4608]{0:T(1024)S(1)} %fusion.91, f32[4608,128]{1,0:T(8,128)} %bitcast.92, f32[]{:T(128)} %constant.241.clone.1..sunk), kind=kCustom, calls=%fused_computation.31.clone.1 | custom fusion | flops 589824 | bytes 786944 | tf_op jit(solution)/shard_map/while/body/eval_jaxpr/scatter-add | solution.py:198
  648.2 8.8 gather_fusion
  677.4 25.3 %scatter_custom_fusion.15 = f32[1536,128]{1,0:T(8,128)S(1)} fusion(s32[4608]{0:T(1024)S(1)} %fusion.91, f32[4608,128]{1,0:T(8,128)S(1)} %bitcast.93, f32[]{:T(128)} %constant.241.clone.1..sunk), kind=kCustom, calls=%fused_computation.33.clone.1 | custom fusion | flops 589824 | bytes 786436 | tf_op jit(solution)/shard_map/while/body/eval_jaxpr/scatter-add | solution.py:197
  705.8 25.6 %scatter_custom_fusion.14 = f32[1536,128]{1,0:T(8,128)S(1)} fusion(s32[4608]{0:T(1024)S(1)} %fusion.91, f32[4608,128]{1,0:T(8,128)} %bitcast.92, f32[]{:T(128)} %constant.241.clone.1..sunk), kind=kCustom, calls=%fused_computation.31.clone.1 | custom fusion | flops 589824 | bytes 786944 | tf_op jit(solution)/shard_map/while/body/eval_jaxpr/scatter-add | solution.py:198
  765.0 25.3 %scatter_custom_fusion.15 = f32[1536,128]{1,0:T(8,128)S(1)} fusion(s32[4608]{0:T(1024)S(1)} %fusion.91, f32[4608,128]{1,0:T(8,128)S(1)} %bitcast.93, f32[]{:T(128)} %constant.241.clone.1..sunk), kind=kCustom, calls=%fused_computation.33.clone.1 | custom fusion | flops 589824 | bytes 786436 | tf_op jit(solution)/shard_map/while/body/eval_jaxpr/scatter-add | solution.py:197
  793.4 25.6 %scatter_custom_fusion.14 = f32[1536,128]{1,0:T(8,128)S(1)} fusion(s32[4608]{0:T(1024)S(1)} %fusion.91, f32[4608,128]{1,0:T(8,128)} %bitcast.92, f32[]{:T(128)} %constant.241.clone.1..sunk), kind=kCustom, calls=%fused_computation.31.clone.1 | custom fusion | flops 589824 | bytes 786944 | tf_op jit(solution)/shard_map/while/body/eval_jaxpr/scatter-add | solution.py:198
  852.5 25.3 %scatter_custom_fusion.15 = f32[1536,128]{1,0:T(8,128)S(1)} fusion(s32[4608]{0:T(1024)S(1)} %fusion.91, f32[4608,128]{1,0:T(8,128)S(1)} %bitcast.93, f32[]{:T(128)} %constant.241.clone.1..sunk), kind=kCustom, calls=%fused_computation.33.clone.1 | custom fusion | flops 589824 | bytes 786436 | tf_op jit(solution)/shard_map/while/body/eval_jaxpr/scatter-add | solution.py:197
  880.9 25.6 %scatter_custom_fusion.14 = f32[1536,128]{1,0:T(8,128)S(1)} fusion(s32[4608]{0:T(1024)S(1)} %fusion.91, f32[4608,128]{1,0:T(8,128)} %bitcast.92, f32[]{:T(128)} %constant.241.clone.1..sunk), kind=kCustom, calls=%fused_computation.31.clone.1 | custom fusion | flops 589824 | bytes 786944 | tf_op jit(solution)/shard_map/while/body/eval_jaxpr/scatter-add | solution.py:198
  940.0 25.3 %scatter_custom_fusion.15 = f32[1536,128]{1,0:T(8,128)S(1)} fusion(s32[4608]{0:T(1024)S(1)} %fusion.91, f32[4608,128]{1,0:T(8,128)S(1)} %bitcast.93, f32[]{:T(128)} %constant.241.clone.1..sunk), kind=kCustom, calls=%fused_computation.33.clone.1 | custom fusion | flops 589824 | bytes 786436 | tf_op jit(solution)/shard_map/while/body/eval_jaxpr/scatter-add | solution.py:197
  968.4 25.6 %scatter_custom_fusion.14 = f32[1536,128]{1,0:T(8,128)S(1)} fusion(s32[4608]{0:T(1024)S(1)} %fusion.91, f32[4608,128]{1,0:T(8,128)} %bitcast.92, f32[]{:T(128)} %constant.241.clone.1..sunk), kind=kCustom, calls=%fused_computation.31.clone.1 | custom fusion | flops 589824 | bytes 786944 | tf_op jit(solution)/shard_map/while/body/eval_jaxpr/scatter-add | solution.py:198
  1009.4 53.3 %collective-permute-done.4 = bf16[2,8,8,8,1280]{4,3,2,1,0:T(8,128)(2,1)} collective-permute-done((bf16[2,8,8,8,1280]{4,3,2,1,0:T(8,128)(2,1)S(1)}, bf16[2,8,8,8,1280]{4,3,2,1,0:T(8,128)(2,1)}, u32[]{:S(2)}, u32[]{:S(2)}) %collective-permute-start.4) | collective-permute-done | bytes 2621472 | tf_op jit(solution)/shard_map/ppermute | solution.py:38
  1087.5 17.2 %collective-permute-done.5 = bf16[2,4,8,8,1280]{4,3,2,1,0:T(8,128)(2,1)} collective-permute-done((bf16[2,4,8,8,1280]{4,3,2,1,0:T(8,128)(2,1)}, bf16[2,4,8,8,1280]{4,3,2,1,0:T(8,128)(2,1)}, u32[]{:S(2)}, u32[]{:S(2)}) %collective-permute-start.5) | collective-permute-done | bytes 1310752 | tf_op jit(solution)/shard_map/ppermute | solution.py:19
  (360 shorter events, 391.6 us)
Async XLA Ops:
  0.6 34.4 %copy-start.6 = (bf16[4,8,8,1280]{3,2,1,0:T(8,128)(2,1)S(1)}, bf16[4,8,8,1280]{3,2,1,0:T(8,128)(2,1)}, u32[]{:S(2)}) copy-start(bf16[4,8,8,1280]{3,2,1,0:T(8,128)(2,1)} %param.27) | copy-start | bytes 1966084
  2.1 33.0 %collective-permute-start = (bf16[2,4,8,8,1280]{4,3,2,1,0:T(8,128)(2,1)S(1)}, bf16[2,4,8,8,1280]{4,3,2,1,0:T(8,128)(2,1)}, u32[]{:S(2)}, u32[]{:S(2)}) collective-permute-start(bf16[2,4,8,8,1280]{4,3,2,1,0:T(8,128)(2,1)S(1)} %pad_maximum_fusion.3), channel_id=1, source_target_pairs={{0,64},{64,0},{1,65},{65,1},{2,66},{66,2},{3,67},{67,3},{4,68},{68... | collective-permute-start | bytes 3932168 | tf_op jit(solution)/shard_map/ppermute | solution.py:19
  6.2 36.8 %copy-start.7 = (s32[1,2,2]{2,1,0:T(2,128)S(1)}, s32[1,2,2]{2,1,0:T(2,128)}, u32[]{:S(2)}) copy-start(s32[1,2,2]{2,1,0:T(2,128)} %param.29) | copy-start | bytes 52
  37.7 60.8 %collective-permute-start.2 = (bf16[2,8,8,8,1280]{4,3,2,1,0:T(8,128)(2,1)S(1)}, bf16[2,8,8,8,1280]{4,3,2,1,0:T(8,128)(2,1)}, u32[]{:S(2)}, u32[]{:S(2)}) collective-permute-start(bf16[2,8,8,8,1280]{4,3,2,1,0:T(8,128)(2,1)S(1)} %fusion.41), channel_id=1, source_target_pairs={{4,0},{8,4},{12,8},{16,12},{20,16},{24,20},{28,24},{32,28},{36,32}... | collective-permute-start | bytes 7864328 | tf_op jit(solution)/shard_map/ppermute | solution.py:30
  43.0 61.2 %collective-permute-start.1 = (bf16[2,8,8,8,1280]{4,3,2,1,0:T(8,128)(2,1)S(1)}, bf16[2,8,8,8,1280]{4,3,2,1,0:T(8,128)(2,1)}, u32[]{:S(2)}, u32[]{:S(2)}) collective-permute-start(bf16[2,8,8,8,1280]{4,3,2,1,0:T(8,128)(2,1)S(1)} %fusion.41), channel_id=1, source_target_pairs={{0,4},{4,8},{8,12},{12,16},{16,20},{20,24},{24,28},{28,32},{32,36}... | collective-permute-start | bytes 7864328 | tf_op jit(solution)/shard_map/ppermute | solution.py:29
  119.9 20.6 %copy-start.3 = (bf16[4,64,1280]{2,1,0:T(8,128)(2,1)}, bf16[4,64,1280]{2,1,0:T(8,128)(2,1)S(1)}, u32[]{:S(2)}) copy-start(bf16[4,64,1280]{2,1,0:T(8,128)(2,1)S(1)} %get-tuple-element.526) | copy-start | bytes 1966084 | tf_op jit(solution)/shard_map/while
  143.1 5.2 copy-start
  180.5 27.0 %copy-start.4 = (bf16[4,64,1280]{2,1,0:T(8,128)(2,1)S(1)}, bf16[4,64,1280]{2,1,0:T(8,128)(2,1)}, u32[]{:S(2)}) copy-start(bf16[4,64,1280]{2,1,0:T(8,128)(2,1)} %copy-done.3) | copy-start | bytes 1966084 | tf_op jit(solution)/shard_map/while
  207.5 20.6 %copy-start.3 = (bf16[4,64,1280]{2,1,0:T(8,128)(2,1)}, bf16[4,64,1280]{2,1,0:T(8,128)(2,1)S(1)}, u32[]{:S(2)}) copy-start(bf16[4,64,1280]{2,1,0:T(8,128)(2,1)S(1)} %get-tuple-element.526) | copy-start | bytes 1966084 | tf_op jit(solution)/shard_map/while
  268.0 27.0 %copy-start.4 = (bf16[4,64,1280]{2,1,0:T(8,128)(2,1)S(1)}, bf16[4,64,1280]{2,1,0:T(8,128)(2,1)}, u32[]{:S(2)}) copy-start(bf16[4,64,1280]{2,1,0:T(8,128)(2,1)} %copy-done.3) | copy-start | bytes 1966084 | tf_op jit(solution)/shard_map/while
  295.0 20.6 %copy-start.3 = (bf16[4,64,1280]{2,1,0:T(8,128)(2,1)}, bf16[4,64,1280]{2,1,0:T(8,128)(2,1)S(1)}, u32[]{:S(2)}) copy-start(bf16[4,64,1280]{2,1,0:T(8,128)(2,1)S(1)} %get-tuple-element.526) | copy-start | bytes 1966084 | tf_op jit(solution)/shard_map/while
  355.6 26.9 %copy-start.4 = (bf16[4,64,1280]{2,1,0:T(8,128)(2,1)S(1)}, bf16[4,64,1280]{2,1,0:T(8,128)(2,1)}, u32[]{:S(2)}) copy-start(bf16[4,64,1280]{2,1,0:T(8,128)(2,1)} %copy-done.3) | copy-start | bytes 1966084 | tf_op jit(solution)/shard_map/while
  382.5 20.6 %copy-start.3 = (bf16[4,64,1280]{2,1,0:T(8,128)(2,1)}, bf16[4,64,1280]{2,1,0:T(8,128)(2,1)S(1)}, u32[]{:S(2)}) copy-start(bf16[4,64,1280]{2,1,0:T(8,128)(2,1)S(1)} %get-tuple-element.526) | copy-start | bytes 1966084 | tf_op jit(solution)/shard_map/while
  443.1 27.0 %copy-start.4 = (bf16[4,64,1280]{2,1,0:T(8,128)(2,1)S(1)}, bf16[4,64,1280]{2,1,0:T(8,128)(2,1)}, u32[]{:S(2)}) copy-start(bf16[4,64,1280]{2,1,0:T(8,128)(2,1)} %copy-done.3) | copy-start | bytes 1966084 | tf_op jit(solution)/shard_map/while
  470.1 20.6 %copy-start.3 = (bf16[4,64,1280]{2,1,0:T(8,128)(2,1)}, bf16[4,64,1280]{2,1,0:T(8,128)(2,1)S(1)}, u32[]{:S(2)}) copy-start(bf16[4,64,1280]{2,1,0:T(8,128)(2,1)S(1)} %get-tuple-element.526) | copy-start | bytes 1966084 | tf_op jit(solution)/shard_map/while
  530.7 26.9 %copy-start.4 = (bf16[4,64,1280]{2,1,0:T(8,128)(2,1)S(1)}, bf16[4,64,1280]{2,1,0:T(8,128)(2,1)}, u32[]{:S(2)}) copy-start(bf16[4,64,1280]{2,1,0:T(8,128)(2,1)} %copy-done.3) | copy-start | bytes 1966084 | tf_op jit(solution)/shard_map/while
  557.6 20.6 %copy-start.3 = (bf16[4,64,1280]{2,1,0:T(8,128)(2,1)}, bf16[4,64,1280]{2,1,0:T(8,128)(2,1)S(1)}, u32[]{:S(2)}) copy-start(bf16[4,64,1280]{2,1,0:T(8,128)(2,1)S(1)} %get-tuple-element.526) | copy-start | bytes 1966084 | tf_op jit(solution)/shard_map/while
  618.2 27.0 %copy-start.4 = (bf16[4,64,1280]{2,1,0:T(8,128)(2,1)S(1)}, bf16[4,64,1280]{2,1,0:T(8,128)(2,1)}, u32[]{:S(2)}) copy-start(bf16[4,64,1280]{2,1,0:T(8,128)(2,1)} %copy-done.3) | copy-start | bytes 1966084 | tf_op jit(solution)/shard_map/while
  645.2 20.6 %copy-start.3 = (bf16[4,64,1280]{2,1,0:T(8,128)(2,1)}, bf16[4,64,1280]{2,1,0:T(8,128)(2,1)S(1)}, u32[]{:S(2)}) copy-start(bf16[4,64,1280]{2,1,0:T(8,128)(2,1)S(1)} %get-tuple-element.526) | copy-start | bytes 1966084 | tf_op jit(solution)/shard_map/while
  705.8 27.0 %copy-start.4 = (bf16[4,64,1280]{2,1,0:T(8,128)(2,1)S(1)}, bf16[4,64,1280]{2,1,0:T(8,128)(2,1)}, u32[]{:S(2)}) copy-start(bf16[4,64,1280]{2,1,0:T(8,128)(2,1)} %copy-done.3) | copy-start | bytes 1966084 | tf_op jit(solution)/shard_map/while
  732.8 20.6 %copy-start.3 = (bf16[4,64,1280]{2,1,0:T(8,128)(2,1)}, bf16[4,64,1280]{2,1,0:T(8,128)(2,1)S(1)}, u32[]{:S(2)}) copy-start(bf16[4,64,1280]{2,1,0:T(8,128)(2,1)S(1)} %get-tuple-element.526) | copy-start | bytes 1966084 | tf_op jit(solution)/shard_map/while
  793.4 27.0 %copy-start.4 = (bf16[4,64,1280]{2,1,0:T(8,128)(2,1)S(1)}, bf16[4,64,1280]{2,1,0:T(8,128)(2,1)}, u32[]{:S(2)}) copy-start(bf16[4,64,1280]{2,1,0:T(8,128)(2,1)} %copy-done.3) | copy-start | bytes 1966084 | tf_op jit(solution)/shard_map/while
  820.3 20.6 %copy-start.3 = (bf16[4,64,1280]{2,1,0:T(8,128)(2,1)}, bf16[4,64,1280]{2,1,0:T(8,128)(2,1)S(1)}, u32[]{:S(2)}) copy-start(bf16[4,64,1280]{2,1,0:T(8,128)(2,1)S(1)} %get-tuple-element.526) | copy-start | bytes 1966084 | tf_op jit(solution)/shard_map/while
  880.9 27.0 %copy-start.4 = (bf16[4,64,1280]{2,1,0:T(8,128)(2,1)S(1)}, bf16[4,64,1280]{2,1,0:T(8,128)(2,1)}, u32[]{:S(2)}) copy-start(bf16[4,64,1280]{2,1,0:T(8,128)(2,1)} %copy-done.3) | copy-start | bytes 1966084 | tf_op jit(solution)/shard_map/while
  907.9 20.6 %copy-start.3 = (bf16[4,64,1280]{2,1,0:T(8,128)(2,1)}, bf16[4,64,1280]{2,1,0:T(8,128)(2,1)S(1)}, u32[]{:S(2)}) copy-start(bf16[4,64,1280]{2,1,0:T(8,128)(2,1)S(1)} %get-tuple-element.526) | copy-start | bytes 1966084 | tf_op jit(solution)/shard_map/while
  968.4 27.0 %copy-start.4 = (bf16[4,64,1280]{2,1,0:T(8,128)(2,1)S(1)}, bf16[4,64,1280]{2,1,0:T(8,128)(2,1)}, u32[]{:S(2)}) copy-start(bf16[4,64,1280]{2,1,0:T(8,128)(2,1)} %copy-done.3) | copy-start | bytes 1966084 | tf_op jit(solution)/shard_map/while
  995.4 5.5 copy-start.1
  1002.3 60.4 %collective-permute-start.4 = (bf16[2,8,8,8,1280]{4,3,2,1,0:T(8,128)(2,1)S(1)}, bf16[2,8,8,8,1280]{4,3,2,1,0:T(8,128)(2,1)}, u32[]{:S(2)}, u32[]{:S(2)}) collective-permute-start(bf16[2,8,8,8,1280]{4,3,2,1,0:T(8,128)(2,1)S(1)} %pad_maximum_fusion.2), channel_id=1, source_target_pairs={{60,0},{0,4},{4,8},{8,12},{12,16},{16,20},{20,24},{24,28},{28,32},... | collective-permute-start | bytes 7864328 | tf_op jit(solution)/shard_map/ppermute | solution.py:38
  1004.0 60.9 %collective-permute-start.3 = (bf16[2,8,8,8,1280]{4,3,2,1,0:T(8,128)(2,1)}, bf16[2,8,8,8,1280]{4,3,2,1,0:T(8,128)(2,1)}, u32[]{:S(2)}, u32[]{:S(2)}) collective-permute-start(bf16[2,8,8,8,1280]{4,3,2,1,0:T(8,128)(2,1)} %pad_maximum_fusion.1), channel_id=1, source_target_pairs={{4,0},{8,4},{12,8},{16,12},{20,16},{24,20},{28,24},{32,28},{36,32}... | collective-permute-start | bytes 7864328 | tf_op jit(solution)/shard_map/ppermute | solution.py:38
  1074.9 9.3 copy-start.5
  1074.9 29.8 %collective-permute-start.5 = (bf16[2,4,8,8,1280]{4,3,2,1,0:T(8,128)(2,1)}, bf16[2,4,8,8,1280]{4,3,2,1,0:T(8,128)(2,1)}, u32[]{:S(2)}, u32[]{:S(2)}) collective-permute-start(bf16[2,4,8,8,1280]{4,3,2,1,0:T(8,128)(2,1)} %pad_maximum_fusion.4), channel_id=1, source_target_pairs={{0,64},{64,0},{1,65},{65,1},{2,66},{66,2},{3,67},{67,3},{4,68},{68... | collective-permute-start | bytes 3932168 | tf_op jit(solution)/shard_map/ppermute | solution.py:19
  1087.5 18.7 %copy-start.2 = (f32[8,8,8,1280]{3,2,1,0:T(8,128)S(1)}, f32[8,8,8,1280]{3,2,1,0:T(8,128)}, u32[]{:S(2)}) copy-start(f32[8,8,8,1280]{3,2,1,0:T(8,128)} %get-tuple-element.391) | copy-start | bytes 7864324
  (9 other events, 46.7 us)
where the time goes:
time: 1110 us
  other arithmetic  559 us (50%)
  local copies, waits for them, and re-layouts  253 us (23%)
  waiting for transfers between devices  149 us (13%)
  matrix products  127 us (11%)
  starting transfers between devices  17.5 us (2%)
    scatter-add x10, other arithmetic, one_head(): value_head_grad = empty.at[index_rows].add(value_block_grad.reshape(-1, HD))  256 us
    scatter-add x10, other arithmetic, one_head(): key_head_grad = empty.at[index_rows].add(key_block_grad.reshape(-1, HD))  253 us
    gather x10, local copies, waits for them, and re-layouts, one_head(): jnp.take(lax.dynamic_slice_in_dim(key_flat, start, HD, 1), flat_index, ax...  87.9 us
    gather x10, local copies, waits for them, and re-layouts, one_head(): jnp.take(lax.dynamic_slice_in_dim(value_flat, start, HD, 1), flat_index,...  87.9 us
    ppermute x2, waiting for transfers between devices, passed_along(): return lax.ppermute(block, axis, route)  53.3 us
    ppermute x2, waiting for transfers between devices, partner(): return lax.ppermute(block, axis, route)  46 us
    ppermute x1, waiting for transfers between devices, extended(): after = lax.ppermute(leading, axis, down)  44 us
    dot_general x10, matrix products, one_head(): jnp.einsum('gqk,gqd->gkd', probs, grad_head, preferred_element_type=jnp.f...  31.3 us
  transfers between devices with their start and end apart: 6, of which 5 were waited for; matrix products, arithmetic and copies ran while one was open for 2% of the time, Pallas kernels for 0%

commit v1 on v0

v1 whole, which is shorter than its diff:
```python
import math

import jax
import jax.numpy as jnp
from jax import lax
from jax.experimental import pallas as pl
from jax.experimental.pallas import tpu as pltpu
from jax.sharding import PartitionSpec as P

HD = 128
TILE = 4
MESH = pl.DeviceIdType.MESH
SCALE = 1.0 / math.sqrt(HD)
EXP_SCALE = SCALE / math.log(2.0)
FAR = -1e30
BF16 = jnp.bfloat16
F32 = jnp.float32
CONTRACT_LAST = (((1,), (1,)), ((), ()))
CONTRACT_FIRST = (((0,), (0,)), ((), ()))


def kernel(
    heads, rows, lats, lons,
    q_in, k_in, v_in, g_in, off_in,
    o_out, dq_out, dk_out, dv_out,
    qb, gb, kv, offs, bias, scores, ob, dqb, back_send, back_recv, own_grad, grad_out,
    load_sem, off_sem, zf_send, zf_recv, xo_send, xo_recv, xp_send, xp_recv,
    xb_send, xb_recv, zb_send, zb_recv, out_sem,
):
    me = lax.axis_index("tm")
    lon = lax.axis_index("lon")
    count = lax.axis_size("lon")
    peer = 1 - me
    sides = (lax.rem(lon + 1, count), lax.rem(lon + count - 1, count))
    full = 2 * rows
    args = (k_in, v_in, q_in, g_in)
    outs = (o_out, dq_out, dk_out, dv_out)

    def columns(owner, j):
        return pl.ds(pl.multiple_of((owner * heads + j) * HD, HD), HD)

    def half(owner):
        return pl.ds(pl.multiple_of(owner * rows, rows), rows)

    def slot(t, j):
        part = kv.at[1, j, t] if t < 2 else (qb.at[j] if t == 2 else gb.at[j])
        return part.at[half(me)]

    def load(t, j):
        return pltpu.make_async_copy(args[t].at[:, columns(me, j)], slot(t, j), load_sem.at[t, j])

    def z_forward(t, j):
        return pltpu.make_async_remote_copy(
            args[t].at[:, columns(peer, j)], slot(t, j), zf_send.at[t, j], zf_recv.at[t, j],
            device_id={"tm": peer}, device_id_type=MESH)

    def x_own(d, t, j):
        return pltpu.make_async_remote_copy(
            args[t].at[:, columns(me, j)], kv.at[2 * d, j, t, half(me)],
            xo_send.at[d, t, j], xo_recv.at[d, t, j],
            device_id={"lon": sides[d]}, device_id_type=MESH)

    def x_peer(d, t, j):
        return pltpu.make_async_remote_copy(
            kv.at[1, j, t, half(peer)], kv.at[2 * d, j, t, half(peer)],
            xp_send.at[d, t, j], xp_recv.at[d, t, j],
            device_id={"lon": sides[d]}, device_id_type=MESH)

    def x_back(d, t, j):
        return pltpu.make_async_remote_copy(
            back_send.at[d, j, t], back_recv.at[d, j, t], xb_send.at[d, t, j], xb_recv.at[d, t, j],
            device_id={"lon": sides[d]}, device_id_type=MESH)

    def result(t, j):
        return (ob.at[j], dqb.at[j], grad_out.at[j, 0], grad_out.at[j, 1])[t]

    def z_back(t, j):
        return pltpu.make_async_remote_copy(
            result(t, j).at[half(peer)], outs[t].at[:, columns(me, j)],
            zb_send.at[t, j], zb_recv.at[t, j],
            device_id={"tm": peer}, device_id_type=MESH)

    def store(t, j):
        return pltpu.make_async_copy(
            result(t, j).at[half(me)], outs[t].at[:, columns(me, j)], out_sem.at[t, j])

    off_load = pltpu.make_async_copy(off_in, offs.at[me], off_sem.at[0])
    off_send = pltpu.make_async_remote_copy(
        off_in, offs.at[me], off_sem.at[1], off_sem.at[2],
        device_id={"tm": peer}, device_id_type=MESH)

    def each(body):
        lax.fori_loop(0, heads, lambda j, c: (body(j), c)[1], 0)

    barrier = pltpu.get_barrier_semaphore()
    pl.semaphore_signal(barrier, inc=1, device_id={"tm": peer}, device_id_type=MESH)
    for side in sides:
        pl.semaphore_signal(barrier, inc=1, device_id={"lon": side}, device_id_type=MESH)
    pl.semaphore_wait(barrier, 3)

    off_send.start()
    off_load.start()

    def begin(j):
        for t in range(2):
            z_forward(t, j).start()
            for d in range(2):
                x_own(d, t, j).start()
        for t in range(4):
            load(t, j).start()

    each(begin)

    def begin_queries(j):
        for t in range(2, 4):
            z_forward(t, j).start()

    each(begin_queries)

    off_load.wait()
    off_send.wait()
    query = lax.broadcasted_iota(jnp.int32, (8, full), 1)
    sub = lax.broadcasted_iota(jnp.int32, (8, full), 0)
    q_frame = query // rows
    q_lat = (query // (lons * TILE)) % 2
    q_lon = (query // TILE) % 2
    centre = q_lon
    for f in range(2):
        for a in range(2):
            for b in range(2):
                value = offs[f, a : a + 1, b : b + 1]
                hit = (q_frame == f) & (q_lat == a) & (q_lon == b)
                centre = centre + jnp.where(hit, value, 0)
    for b in range(3):
        gap = sub // TILE + (2 * b - 2) - centre
        bias[b] = jnp.where(jnp.abs(gap) <= 1, 0.0, FAR).astype(F32)

    def forward_peer(j):
        for t in range(2):
            z_forward(t, j).wait_recv()
            for d in range(2):
                x_peer(d, t, j).start()

    each(forward_peer)

    groups = full // 8

    def head(j):
        for t in range(4):
            load(t, j).wait()
        for t in range(2, 4):
            z_forward(t, j).wait_recv()
        for d in range(2):
            for t in range(2):
                x_own(d, t, j).wait_recv()
                x_peer(d, t, j).wait_recv()
        q = qb[j]
        g = gb[j]
        peak = None
        for b in range(3):
            s = lax.dot_general(kv[b, j, 0], q, CONTRACT_LAST, preferred_element_type=F32)
            s = s.reshape(groups, 8, full) + bias[b]
            scores[b] = s.reshape(full, full)
            top = jnp.max(s, axis=0)
            peak = top if peak is None else jnp.maximum(peak, top)
        peak = jnp.max(peak, axis=0, keepdims=True)
        total = jnp.zeros((8, full), F32)
        out_t = jnp.zeros((HD, full), F32)
        for b in range(3):
            p = jnp.exp2((scores[b] - peak) * EXP_SCALE)
            scores[b] = p
            total = total + jnp.sum(p.reshape(groups, 8, full), axis=0)
            out_t = out_t + lax.dot_general(
                kv[b, j, 1], p.astype(BF16), CONTRACT_FIRST, preferred_element_type=F32)
        inverse = 1.0 / jnp.sum(total, axis=0, keepdims=True)
        out_t = out_t * inverse
        g_t = g.astype(F32).T
        ob[j] = out_t.T.astype(BF16)
        delta = jnp.sum(out_t.astype(BF16).astype(F32) * g_t, axis=0, keepdims=True)
        dq_t = jnp.zeros((HD, full), F32)
        for b in (0, 2, 1):
            probs = scores[b] * inverse
            dp = lax.dot_general(kv[b, j, 1], g, CONTRACT_LAST, preferred_element_type=F32)
            ds = (probs * (dp - delta)).astype(BF16)
            dk = jnp.dot(ds, q, preferred_element_type=F32) * SCALE
            dv = jnp.dot(probs.astype(BF16), g, preferred_element_type=F32)
            dq_t = dq_t + lax.dot_general(
                kv[b, j, 0], ds, CONTRACT_FIRST, preferred_element_type=F32)
            if b == 1:
                own_grad[j, 0] = dk
                own_grad[j, 1] = dv
            else:
                back_send[1 - b // 2, j, 0] = dk.astype(BF16)
                back_send[1 - b // 2, j, 1] = dv.astype(BF16)
        dqb[j] = (dq_t * SCALE).T.astype(BF16)
        for t in range(2):
            for d in range(2):
                x_back(d, t, j).start()
        for t in range(2):
            z_back(t, j).start()
            store(t, j).start()

    each(head)

    def finish(j):
        for t in range(2):
            for d in range(2):
                x_back(d, t, j).wait_recv()
            grad = own_grad[j, t] + back_recv[0, j, t].astype(F32) + back_recv[1, j, t].astype(F32)
            grad_out[j, t] = grad.astype(BF16)
        for t in range(2, 4):
            z_back(t, j).start()
            store(t, j).start()

    each(finish)

    def drain(j):
        for t in range(4):
            z_forward(t, j).wait_send()
            z_back(t, j).wait_send()
            z_back(t, j).wait_recv()
            store(t, j).wait()
        for d in range(2):
            for t in range(2):
                x_own(d, t, j).wait_send()
                x_peer(d, t, j).wait_send()
                x_back(d, t, j).wait_send()

    each(drain)


def on_device(query_rows, key_rows, value_rows, out_grad, window_offsets):
    frames, lats, lons, width = query_rows.shape
    heads = width // HD // 2
    rows = frames * lats * lons
    full = 2 * rows
    flat = lambda x: x.reshape(rows, width)
    offs = jnp.pad(window_offsets[0], ((0, 6), (0, 126)))
    sem = pltpu.SemaphoreType.DMA
    body = lambda *refs: kernel(heads, rows, lats, lons, *refs)
    outs = pl.pallas_call(
        body,
        out_shape=[jax.ShapeDtypeStruct((rows, width), BF16)] * 4,
        in_specs=[pl.BlockSpec(memory_space=pl.ANY)] * 5,
        out_specs=[pl.BlockSpec(memory_space=pl.ANY)] * 4,
        scratch_shapes=[
            pltpu.VMEM((heads, full, HD), BF16),
            pltpu.VMEM((heads, full, HD), BF16),
            pltpu.VMEM((3, heads, 2, full, HD), BF16),
            pltpu.VMEM((2, 8, 128), jnp.int32),
            pltpu.VMEM((3, 8, full), F32),
            pltpu.VMEM((3, full, full), F32),
            pltpu.VMEM((heads, full, HD), BF16),
            pltpu.VMEM((heads, full, HD), BF16),
            pltpu.VMEM((2, heads, 2, full, HD), BF16),
            pltpu.VMEM((2, heads, 2, full, HD), BF16),
            pltpu.VMEM((heads, 2, full, HD), F32),
            pltpu.VMEM((heads, 2, full, HD), BF16),
            sem((4, heads)),
            sem((3,)),
            sem((4, heads)),
            sem((4, heads)),
            sem((2, 2, heads)),
            sem((2, 2, heads)),
            sem((2, 2, heads)),
            sem((2, 2, heads)),
            sem((2, 2, heads)),
            sem((2, 2, heads)),
            sem((4, heads)),
            sem((4, heads)),
            sem((4, heads)),
        ],
        compiler_params=pltpu.CompilerParams(collective_id=0, has_side_effects=True),
    )(flat(query_rows), flat(key_rows), flat(value_rows), flat(out_grad), offs)
    return tuple(x.reshape(frames, lats, lons, width) for x in outs)


def solution(mesh):
    rows = P("tm", None, "lon", "head")
    return jax.shard_map(
        on_device,
        mesh=mesh,
        in_specs=(rows, rows, rows, rows, P("tm", None, "lon")),
        out_specs=(rows, rows, rows, rows),
        check_vma=False,
    )
```

time: 1110 us -> 79.8 us (0.07)
  other arithmetic: 559 us -> 0 us
  local copies, waits for them, and re-layouts: 253 us -> 6.78 us
  waiting for transfers between devices: 149 us -> 0 us
  matrix products: 127 us -> 0 us
  Pallas kernels: 0 us -> 72.1 us
  starting transfers between devices: 17.5 us -> 0 us
    scatter-add x20 -> x0, other arithmetic: 509 us -> none  [the longest x10 256 us: one_head(): value_head_grad = empty.at[index_rows].add(value_block_grad.reshape(-1, HD))]
    gather x20 -> x0, local copies, waits for them, and re-layouts: 176 us -> none  [the longest x10 87.9 us: one_head(): jnp.take(lax.dynamic_slice_in_dim(key_flat, start, HD, 1), flat_index, ax...]
    ppermute x6 -> x0, waiting for transfers between devices: 149 us -> none  [the longest x2 53.3 us: passed_along(): return lax.ppermute(block, axis, route)]
    dot_general x60 -> x0, matrix products: 127 us -> none  [the longest x10 31.3 us: one_head(): jnp.einsum('gqk,gqd->gkd', probs, grad_head, preferred_element_type=jnp.f...]
    pallas_call x0 -> x1, Pallas kernels: none -> 72.1 us  [on_device(): pl.pallas_call(body, out_shape=[jax.ShapeDtypeStruct((rows, width), BF16)...]
    reshape x13 -> x0, local copies, waits for them, and re-layouts: 20.8 us -> none  [the longest x4 7.1 us: to_groups(): array.reshape(frame_tiles, TILE, lat_tiles, TILE, lon_tiles, TILE, width)]
    dynamic_slice x20 -> x0, local copies, waits for them, and re-layouts: 20.6 us -> none  [the longest x10 10.3 us: one_head(): lax.dynamic_slice_in_dim(key_flat, start, HD, 1)]
    ppermute x6 -> x0, starting transfers between devices: 17.5 us -> none  [the longest x2 6.76 us: partner(): return lax.ppermute(block, axis, route)]
  transfers between devices with their start and end apart: 6 -> 0, of which waited for: 5 -> 0; matrix products, arithmetic and copies ran while one was open for 2% -> 0% of each run, Pallas kernels for 0% -> 0%
where the time goes in v1:
time: 79.8 us; the launch traced here: 79.5 us
  Pallas kernels  72.1 us (90%)
  local copies, waits for them, and re-layouts  6.78 us (8%)
    pallas_call x1, Pallas kernels, on_device(): pl.pallas_call(body, out_shape=[jax.ShapeDtypeStruct((rows, width), BF16)...  72.1 us
    unnamed x12, local copies, waits for them, and re-layouts  6.19 us

profile of v1, /device:TPU:0, one launch (start us, length us, event | category | flops | bytes accessed | tf_op | source)
XLA Modules:
  0.0 79.5 jit_solution(958403216001242090)
XLA Ops:
  0.6 0.0 copy-start.3
  0.6 0.7 copy-done.3
  1.3 0.6 pad.4.refs_4_
  1.9 72.1 %shard_map.84 = (bf16[256,1280]{1,0:T(8,128)(2,1)}, bf16[256,1280]{1,0:T(8,128)(2,1)}, bf16[256,1280]{1,0:T(8,128)(2,1)}, bf16[256,1280]{1,0:T(8,128)(2,1)}) custom-call(bf16[256,1280]{1,0:T(8,128)(2,1)} %bitcast.9, bf16[256,1280]{1,0:T(8,128)(2,1)} %bitcast.10, bf16[256,1280]{1,0:T(8,128)(2,1)} %bitcast.11, bf16[256,1280]{1,0:T(8,128)(2,1)} %bitcast.12, ...), custom_call_target="tpu_custom_call" | custom-call | tf_op jit(solution)/shard_map/pallas_call | solution.py:241
  74.0 0.0 copy-start.2
  74.0 2.0 %copy.13 = bf16[4,8,8,1280]{3,2,1,0:T(8,128)(2,1)} copy(bf16[4,8,8,1280]{3,2,1,0:T(8,128)(2,1)} %bitcast.16) | data formatting | bytes 1310720
  76.1 0.0 copy-done.2
  76.1 0.0 copy-start.1
  76.1 0.8 %copy.14 = bf16[4,8,8,1280]{3,2,1,0:T(8,128)(2,1)} copy(bf16[4,8,8,1280]{3,2,1,0:T(8,128)(2,1)S(1)} %bitcast.15) | data formatting | bytes 1310720
  76.9 0.5 copy-done.1
  77.4 0.0 copy-start
  77.4 0.8 %copy.15 = bf16[4,8,8,1280]{3,2,1,0:T(8,128)(2,1)} copy(bf16[4,8,8,1280]{3,2,1,0:T(8,128)(2,1)S(1)} %bitcast.14) | data formatting | bytes 1310720
  78.2 0.5 copy-done
  78.7 0.8 %copy.16 = bf16[4,8,8,1280]{3,2,1,0:T(8,128)(2,1)} copy(bf16[4,8,8,1280]{3,2,1,0:T(8,128)(2,1)S(1)} %bitcast.13) | data formatting | bytes 1310720
Async XLA Ops:
  0.6 0.7 copy-start.3
  74.0 2.0 %copy-start.2 = (bf16[256,1280]{1,0:T(8,128)(2,1)S(1)}, bf16[256,1280]{1,0:T(8,128)(2,1)}, u32[]{:S(2)}) copy-start(bf16[256,1280]{1,0:T(8,128)(2,1)} %get-tuple-element.9) | copy-start | bytes 1966084
  76.1 1.3 %copy-start.1 = (bf16[256,1280]{1,0:T(8,128)(2,1)S(1)}, bf16[256,1280]{1,0:T(8,128)(2,1)}, u32[]{:S(2)}) copy-start(bf16[256,1280]{1,0:T(8,128)(2,1)} %get-tuple-element.10) | copy-start | bytes 1966084
  77.4 1.3 %copy-start = (bf16[256,1280]{1,0:T(8,128)(2,1)S(1)}, bf16[256,1280]{1,0:T(8,128)(2,1)}, u32[]{:S(2)}) copy-start(bf16[256,1280]{1,0:T(8,128)(2,1)} %get-tuple-element.11) | copy-start | bytes 1966084

commit v2 on v1

--- a/solution.py
+++ b/solution.py
@@ -66,9 +66,11 @@
             xp_send.at[d, t, j], xp_recv.at[d, t, j],
             device_id={"lon": sides[d]}, device_id_type=MESH)
 
-    def x_back(d, t, j):
-        return pltpu.make_async_remote_copy(
-            back_send.at[d, j, t], back_recv.at[d, j, t], xb_send.at[d, t, j], xb_recv.at[d, t, j],
+    def x_back(h, d, t, j):
+        part = half((peer, me)[h])
+        return pltpu.make_async_remote_copy(
+            back_send.at[d, j, t, part], back_recv.at[d, j, t, part],
+            xb_send.at[h, d, t, j], xb_recv.at[h, d, t, j],
             device_id={"lon": sides[d]}, device_id_type=MESH)
 
     def result(t, j):
@@ -84,9 +86,9 @@
         return pltpu.make_async_copy(
             result(t, j).at[half(me)], outs[t].at[:, columns(me, j)], out_sem.at[t, j])
 
-    off_load = pltpu.make_async_copy(off_in, offs.at[me], off_sem.at[0])
+    off_load = pltpu.make_async_copy(off_in.at[0], offs.at[me], off_sem.at[0])
     off_send = pltpu.make_async_remote_copy(
-        off_in, offs.at[me], off_sem.at[1], off_sem.at[2],
+        off_in.at[0], offs.at[me], off_sem.at[1], off_sem.at[2],
         device_id={"tm": peer}, device_id_type=MESH)
 
     def each(body):
@@ -195,24 +197,43 @@
         dqb[j] = (dq_t * SCALE).T.astype(BF16)
         for t in range(2):
             for d in range(2):
-                x_back(d, t, j).start()
+                x_back(0, d, t, j).start()
         for t in range(2):
             z_back(t, j).start()
             store(t, j).start()
 
     each(head)
 
-    def finish(j):
-        for t in range(2):
-            for d in range(2):
-                x_back(d, t, j).wait_recv()
-            grad = own_grad[j, t] + back_recv[0, j, t].astype(F32) + back_recv[1, j, t].astype(F32)
-            grad_out[j, t] = grad.astype(BF16)
+    def return_own(j):
+        for t in range(2):
+            for d in range(2):
+                x_back(1, d, t, j).start()
+
+    each(return_own)
+
+    def add_up(h, j):
+        part = half((peer, me)[h])
+        for t in range(2):
+            for d in range(2):
+                x_back(h, d, t, j).wait_recv()
+            grad = own_grad[j, t, part]
+            for d in range(2):
+                grad = grad + back_recv[d, j, t, part].astype(F32)
+            grad_out[j, t, part] = grad.astype(BF16)
+
+    def finish_peer(j):
+        add_up(0, j)
         for t in range(2, 4):
             z_back(t, j).start()
+
+    each(finish_peer)
+
+    def finish_own(j):
+        add_up(1, j)
+        for t in range(2, 4):
             store(t, j).start()
 
-    each(finish)
+    each(finish_own)
 
     def drain(j):
         for t in range(4):
@@ -224,9 +245,20 @@
             for t in range(2):
                 x_own(d, t, j).wait_send()
                 x_peer(d, t, j).wait_send()
-                x_back(d, t, j).wait_send()
+                for h in range(2):
+                    x_back(h, d, t, j).wait_send()
 
     each(drain)
+
+
+def move(*refs):
+    count = len(refs) // 2
+    sems = refs[-1]
+    copies = [pltpu.make_async_copy(refs[i], refs[count + i], sems.at[i]) for i in range(4)]
+    for copy in copies:
+        copy.start()
+    for copy in copies:
+        copy.wait()
 
 
 def on_device(query_rows, key_rows, value_rows, out_grad, window_offsets):
@@ -235,19 +267,18 @@
     rows = frames * lats * lons
     full = 2 * rows
     flat = lambda x: x.reshape(rows, width)
-    offs = jnp.pad(window_offsets[0], ((0, 6), (0, 126)))
     sem = pltpu.SemaphoreType.DMA
     body = lambda *refs: kernel(heads, rows, lats, lons, *refs)
     outs = pl.pallas_call(
         body,
-        out_shape=[jax.ShapeDtypeStruct((rows, width), BF16)] * 4,
+        out_shape=[pltpu.VMEM((rows, width), BF16)] * 4,
         in_specs=[pl.BlockSpec(memory_space=pl.ANY)] * 5,
         out_specs=[pl.BlockSpec(memory_space=pl.ANY)] * 4,
         scratch_shapes=[
             pltpu.VMEM((heads, full, HD), BF16),
             pltpu.VMEM((heads, full, HD), BF16),
             pltpu.VMEM((3, heads, 2, full, HD), BF16),
-            pltpu.VMEM((2, 8, 128), jnp.int32),
+            pltpu.VMEM((2, 2, 2), jnp.int32),
             pltpu.VMEM((3, 8, full), F32),
             pltpu.VMEM((3, full, full), F32),
             pltpu.VMEM((heads, full, HD), BF16),
@@ -264,14 +295,22 @@
             sem((2, 2, heads)),
             sem((2, 2, heads)),
             sem((2, 2, heads)),
-            sem((2, 2, heads)),
-            sem((2, 2, heads)),
+            sem((2, 2, 2, heads)),
+            sem((2, 2, 2, heads)),
             sem((4, heads)),
             sem((4, heads)),
             sem((4, heads)),
         ],
         compiler_params=pltpu.CompilerParams(collective_id=0, has_side_effects=True),
-    )(flat(query_rows), flat(key_rows), flat(value_rows), flat(out_grad), offs)
+    )(flat(query_rows), flat(key_rows), flat(value_rows), flat(out_grad), window_offsets)
+    outs = pl.pallas_call(
+        move,
+        out_shape=[jax.ShapeDtypeStruct((rows, width), BF16)] * 4,
+        in_specs=[pl.BlockSpec(memory_space=pl.ANY)] * 4,
+        out_specs=[pl.BlockSpec(memory_space=pl.ANY)] * 4,
+        scratch_shapes=[sem((4,))],
+        compiler_params=pltpu.CompilerParams(vmem_limit_bytes=1 << 20),
+    )(*outs)
     return tuple(x.reshape(frames, lats, lons, width) for x in outs)
 
 

time: 79.8 us -> 71.2 us (0.89)
  local copies, waits for them, and re-layouts: 6.78 us -> 0 us
  Pallas kernels: 72.1 us -> 70.4 us
    unnamed x12 -> x0, local copies, waits for them, and re-layouts: 6.19 us -> none
    pallas_call x1 -> x2, Pallas kernels: 72.1 us -> 70.4 us  [the longest x1 68.9 us: on_device(): pl.pallas_call(body, out_shape=[pltpu.VMEM((rows, width), BF16)] * 4, in_...]
where the time goes in v2:
time: 71.2 us; the launch traced here: 71.1 us
  Pallas kernels  70.4 us (99%)
    pallas_call x1, Pallas kernels, on_device(): pl.pallas_call(body, out_shape=[pltpu.VMEM((rows, width), BF16)] * 4, in_...  68.9 us
    pallas_call x1, Pallas kernels, on_device(): pl.pallas_call(move, out_shape=[jax.ShapeDtypeStruct((rows, width), BF16)...  1.52 us

profile of v2, /device:TPU:0, one launch (start us, length us, event | category | flops | bytes accessed | tf_op | source)
XLA Modules:
  0.0 71.1 jit_solution(6331425157324488824)
XLA Ops:
  0.6 68.9 %shard_map.84 = (bf16[256,1280]{1,0:T(8,128)(2,1)S(1)}, bf16[256,1280]{1,0:T(8,128)(2,1)S(1)}, bf16[256,1280]{1,0:T(8,128)(2,1)S(1)}, bf16[256,1280]{1,0:T(8,128)(2,1)S(1)}) custom-call(bf16[256,1280]{1,0:T(8,128)(2,1)} %bitcast.8, bf16[256,1280]{1,0:T(8,128)(2,1)} %bitcast.9, bf16[256,1280]{1,0:T(8,128)(2,1)} %bitcast.10, bf16[256,1280]{1,0:T(8,128)(2,1)} %bitcast.11, ...), custom_call_target="tpu_custom_call" | custom-call | tf_op jit(solution)/shard_map/pallas_call | solution.py:272
  69.6 1.5 %shard_map.85 = (bf16[256,1280]{1,0:T(8,128)(2,1)}, bf16[256,1280]{1,0:T(8,128)(2,1)}, bf16[256,1280]{1,0:T(8,128)(2,1)}, bf16[256,1280]{1,0:T(8,128)(2,1)}) custom-call(bf16[256,1280]{1,0:T(8,128)(2,1)S(1)} %get-tuple-element.12.refs_0_, bf16[256,1280]{1,0:T(8,128)(2,1)S(1)} %get-tuple-element.13.refs_1_, bf16[256,1280]{1,0:T(8,128)(2,1)S(1)} %get-tuple-element.14.refs_2_, ...), custom_call_target="tpu_custom_call" | custom-call | tf_op jit(solution)/shard_map/pallas_call | solution.py:306

commit v3 on v2

v3 whole, which is shorter than its diff:
```python
import math

import jax
import jax.numpy as jnp
from jax import lax
from jax.experimental import pallas as pl
from jax.experimental.pallas import tpu as pltpu
from jax.sharding import PartitionSpec as P

HD = 128
TILE = 4
MESH = pl.DeviceIdType.MESH
SCALE = 1.0 / math.sqrt(HD)
EXP_SCALE = SCALE / math.log(2.0)
FAR = -1e30
BF16 = jnp.bfloat16
F32 = jnp.float32
CONTRACT_LAST = (((1,), (1,)), ((), ()))
CONTRACT_FIRST = (((0,), (0,)), ((), ()))


def kernel(
    heads, rows, lats, lons,
    q_in, k_in, v_in, g_in, off_in,
    out,
    qg, kv, offs, bias, scores, result, back_send, back_recv, own_grad,
    load_sem, off_sem, zf_send, zf_recv, xo_send, xo_recv, xf_send, xf_recv, xb_send, xb_recv,
    zb_send, zb_recv, out_sem,
):
    me = lax.axis_index("tm")
    lon = lax.axis_index("lon")
    count = lax.axis_size("lon")
    peer = 1 - me
    sides = (lax.rem(lon + 1, count), lax.rem(lon + count - 1, count))
    full = 2 * rows
    args = (k_in, v_in, q_in, g_in)

    def columns(owner, j):
        return pl.ds(pl.multiple_of((owner * heads + j) * HD, HD), HD)

    def half(owner):
        return pl.ds(pl.multiple_of(owner * rows, rows), rows)

    def slot(t, j):
        place = kv.at[1, j, t] if t < 2 else qg.at[j, t - 2]
        return place.at[half(me)]

    def load(t, j):
        return pltpu.make_async_copy(args[t].at[:, columns(me, j)], slot(t, j), load_sem.at[t, j])

    def z_forward(t, j):
        return pltpu.make_async_remote_copy(
            args[t].at[:, columns(peer, j)], slot(t, j), zf_send.at[t, j], zf_recv.at[t, j],
            device_id={"tm": peer}, device_id_type=MESH)

    def x_own(d):
        return pltpu.make_async_remote_copy(
            kv.at[1, :, :, half(me)], kv.at[2 * d, :, :, half(me)],
            xo_send.at[d], xo_recv.at[d],
            device_id={"lon": sides[d]}, device_id_type=MESH)

    def x_peer(d, j):
        return pltpu.make_async_remote_copy(
            kv.at[1, j, :, half(peer)], kv.at[2 * d, j, :, half(peer)],
            xf_send.at[d, j], xf_recv.at[d, j],
            device_id={"lon": sides[d]}, device_id_type=MESH)

    def x_back(h, d, j):
        return pltpu.make_async_remote_copy(
            back_send.at[d, j, :, half((peer, me)[h])], back_recv.at[h, d, j],
            xb_send.at[h, d, j], xb_recv.at[h, d, j],
            device_id={"lon": sides[d]}, device_id_type=MESH)

    def z_back(pair, j):
        return pltpu.make_async_remote_copy(
            result.at[j, pl.ds(2 * pair, 2), half(peer)],
            out.at[pl.ds(2 * pair, 2), :, columns(me, j)],
            zb_send.at[pair, j], zb_recv.at[pair, j],
            device_id={"tm": peer}, device_id_type=MESH)

    def store(j):
        return pltpu.make_async_copy(
            result.at[j, pl.ds(0, 2), half(me)],
            out.at[pl.ds(0, 2), :, columns(me, j)], out_sem.at[j])

    off_load = pltpu.make_async_copy(off_in.at[0], offs.at[me], off_sem.at[0])
    off_send = pltpu.make_async_remote_copy(
        off_in.at[0], offs.at[me], off_sem.at[1], off_sem.at[2],
        device_id={"tm": peer}, device_id_type=MESH)

    def each(body):
        lax.fori_loop(0, heads, lambda j, c: (body(j), c)[1], 0)

    barrier = pltpu.get_barrier_semaphore()
    pl.semaphore_signal(barrier, inc=1, device_id={"tm": peer}, device_id_type=MESH)
    for side in sides:
        pl.semaphore_signal(barrier, inc=1, device_id={"lon": side}, device_id_type=MESH)


    def begin(j):
        for t in range(2):
            load(t, j).start()

    def begin_keys(j):
        for t in range(2):
            z_forward(t, j).start()

    def begin_queries(j):
        for t in range(2, 4):
            z_forward(t, j).start()
            load(t, j).start()

    def wait_keys(j):
        for t in range(2):
            load(t, j).wait()

    each(begin)
    pl.semaphore_wait(barrier, 3)
    each(begin_keys)
    each(wait_keys)
    for d in range(2):
        x_own(d).start()
    off_send.start()
    off_load.start()
    each(begin_queries)
    off_load.wait()
    off_send.wait()
    query = lax.broadcasted_iota(jnp.int32, (8, full), 1)
    sub = lax.broadcasted_iota(jnp.int32, (8, full), 0)
    q_frame = query // rows
    q_lat = (query // (lons * TILE)) % 2
    q_lon = (query // TILE) % 2
    centre = q_lon
    for f in range(2):
        for a in range(2):
            for b in range(2):
                value = offs[f, a : a + 1, b : b + 1]
                hit = (q_frame == f) & (q_lat == a) & (q_lon == b)
                centre = centre + jnp.where(hit, value, 0)
    for b in range(3):
        gap = sub // TILE + (2 * b - 2) - centre
        bias[b] = jnp.where(jnp.abs(gap) <= 1, 0.0, FAR).astype(F32)

    def forward_peer(j):
        for t in range(2):
            z_forward(t, j).wait_recv()
        for d in range(2):
            x_peer(d, j).start()

    each(forward_peer)

    groups = full // 8
    for d in range(2):
        x_own(d).wait_recv()

    def head(j):
        for t in range(2, 4):
            load(t, j).wait()
            z_forward(t, j).wait_recv()
        for d in range(2):
            x_peer(d, j).wait_recv()
        q = qg[j, 0]
        g = qg[j, 1]
        peak = None
        for b in range(3):
            s = lax.dot_general(kv[b, j, 0], q, CONTRACT_LAST, preferred_element_type=F32)
            s = s.reshape(groups, 8, full) + bias[b]
            scores[b] = s.reshape(full, full)
            top = jnp.max(s, axis=0)
            peak = top if peak is None else jnp.maximum(peak, top)
        peak = jnp.max(peak, axis=0, keepdims=True)
        total = jnp.zeros((8, full), F32)
        out_t = jnp.zeros((HD, full), F32)
        for b in range(3):
            p = jnp.exp2((scores[b] - peak) * EXP_SCALE)
            scores[b] = p
            total = total + jnp.sum(p.reshape(groups, 8, full), axis=0)
            out_t = out_t + lax.dot_general(
                kv[b, j, 1], p.astype(BF16), CONTRACT_FIRST, preferred_element_type=F32)
        inverse = 1.0 / jnp.sum(total, axis=0, keepdims=True)
        out_t = out_t * inverse
        g_t = g.astype(F32).T
        result[j, 0] = out_t.T.astype(BF16)
        delta = jnp.sum(out_t.astype(BF16).astype(F32) * g_t, axis=0, keepdims=True)
        dq_t = jnp.zeros((HD, full), F32)
        for b in (0, 2, 1):
            probs = scores[b] * inverse
            dp = lax.dot_general(kv[b, j, 1], g, CONTRACT_LAST, preferred_element_type=F32)
            ds = (probs * (dp - delta)).astype(BF16)
            dk = jnp.dot(ds, q, preferred_element_type=F32) * SCALE
            dv = jnp.dot(probs.astype(BF16), g, preferred_element_type=F32)
            dq_t = dq_t + lax.dot_general(
                kv[b, j, 0], ds, CONTRACT_FIRST, preferred_element_type=F32)
            if b == 1:
                own_grad[j, 0] = dk
                own_grad[j, 1] = dv
            else:
                back_send[1 - b // 2, j, 0] = dk.astype(BF16)
                back_send[1 - b // 2, j, 1] = dv.astype(BF16)
        result[j, 1] = (dq_t * SCALE).T.astype(BF16)
        for d in range(2):
            x_back(0, d, j).start()
        z_back(0, j).start()
        store(j).start()

    each(head)

    def return_own(j):
        for d in range(2):
            x_back(1, d, j).start()

    each(return_own)

    def add_up(h, j, t):
        grad = own_grad[j, t, half((peer, me)[h])]
        for d in range(2):
            grad = grad + back_recv[h, d, j, t].astype(F32)
        return grad.astype(BF16)

    def finish_peer(j):
        for d in range(2):
            x_back(0, d, j).wait_recv()
        for t in range(2):
            result[j, 2 + t, half(peer)] = add_up(0, j, t)
        z_back(1, j).start()

    each(finish_peer)

    def finish_own(j):
        for d in range(2):
            x_back(1, d, j).wait_recv()
        for t in range(2):
            out[2 + t, :, columns(me, j)] = add_up(1, j, t)

    each(finish_own)

    for d in range(2):
        x_own(d).wait_send()

    def drain(j):
        for t in range(4):
            z_forward(t, j).wait_send()
        for pair in range(2):
            z_back(pair, j).wait_send()
            z_back(pair, j).wait_recv()
        store(j).wait()
        for d in range(2):
            x_peer(d, j).wait_send()
            for h in range(2):
                x_back(h, d, j).wait_send()

    each(drain)


def move(packed, *refs):
    outs, sems = refs[:-1], refs[-1]
    copies = [
        pltpu.make_async_copy(packed.at[i], out, sems.at[i]) for i, out in enumerate(outs)
    ]
    for copy in copies:
        copy.start()
    for copy in copies:
        copy.wait()


def on_device(query_rows, key_rows, value_rows, out_grad, window_offsets):
    frames, lats, lons, width = query_rows.shape
    heads = width // HD // 2
    rows = frames * lats * lons
    full = 2 * rows
    flat = lambda x: x.reshape(rows, width)
    sem = pltpu.SemaphoreType.DMA
    body = lambda *refs: kernel(heads, rows, lats, lons, *refs)
    packed = pl.pallas_call(
        body,
        out_shape=pltpu.VMEM((4, rows, width), BF16),
        in_specs=[pl.BlockSpec(memory_space=pl.ANY)] * 5,
        out_specs=pl.BlockSpec(memory_space=pltpu.VMEM),
        scratch_shapes=[
            pltpu.VMEM((heads, 2, full, HD), BF16),
            pltpu.VMEM((3, heads, 2, full, HD), BF16),
            pltpu.VMEM((2, 2, 2), jnp.int32),
            pltpu.VMEM((3, 8, full), F32),
            pltpu.VMEM((3, full, full), F32),
            pltpu.VMEM((heads, 4, full, HD), BF16),
            pltpu.VMEM((2, heads, 2, full, HD), BF16),
            pltpu.VMEM((2, 2, heads, 2, rows, HD), BF16),
            pltpu.VMEM((heads, 2, full, HD), F32),
            sem((4, heads)),
            sem((3,)),
            sem((4, heads)),
            sem((4, heads)),
            sem((2,)),
            sem((2,)),
            sem((2, heads)),
            sem((2, heads)),
            sem((2, 2, heads)),
            sem((2, 2, heads)),
            sem((2, heads)),
            sem((2, heads)),
            sem((heads,)),
        ],
        compiler_params=pltpu.CompilerParams(collective_id=0, has_side_effects=True),
    )(flat(query_rows), flat(key_rows), flat(value_rows), flat(out_grad), window_offsets)
    outs = pl.pallas_call(
        move,
        out_shape=[jax.ShapeDtypeStruct((rows, width), BF16)] * 4,
        in_specs=[pl.BlockSpec(memory_space=pl.ANY)],
        out_specs=[pl.BlockSpec(memory_space=pl.ANY)] * 4,
        scratch_shapes=[sem((4,))],
        compiler_params=pltpu.CompilerParams(vmem_limit_bytes=1 << 20),
    )(packed)
    return tuple(x.reshape(frames, lats, lons, width) for x in outs)


def solution(mesh):
    rows = P("tm", None, "lon", "head")
    return jax.shard_map(
        on_device,
        mesh=mesh,
        in_specs=(rows, rows, rows, rows, P("tm", None, "lon")),
        out_specs=(rows, rows, rows, rows),
        check_vma=False,
    )
```

time: 71.2 us -> 70.8 us (level)
  no operation moved by 1% of the time
where the time goes in v3:
time: 70.8 us; the launch traced here: 70.6 us
  Pallas kernels  69.9 us (99%)
    pallas_call x1, Pallas kernels, on_device(): pl.pallas_call(body, out_shape=pltpu.VMEM((4, rows, width), BF16), in_spe...  68.4 us
    pallas_call x1, Pallas kernels, on_device(): pl.pallas_call(move, out_shape=[jax.ShapeDtypeStruct((rows, width), BF16)...  1.52 us

profile of v3, /device:TPU:0, one launch (start us, length us, event | category | flops | bytes accessed | tf_op | source)
XLA Modules:
  0.0 70.6 jit_solution(7211207214777785453)
XLA Ops:
  0.6 68.4 %shard_map.84.packed = bf16[4,256,1280]{2,1,0:T(8,128)(2,1)S(1)} custom-call(bf16[256,1280]{1,0:T(8,128)(2,1)} %bitcast.8, bf16[256,1280]{1,0:T(8,128)(2,1)} %bitcast.9, bf16[256,1280]{1,0:T(8,128)(2,1)} %bitcast.10, bf16[256,1280]{1,0:T(8,128)(2,1)} %bitcast.11, s32[1,2,2]{2,1,0:T(2,128)} %refs_4_.1), custom_call_target="tpu_custom_call" | custom-call | tf_op jit(solution)/shard_map/pallas_call | solution.py:274
  69.1 1.5 %shard_map.85 = (bf16[256,1280]{1,0:T(8,128)(2,1)}, bf16[256,1280]{1,0:T(8,128)(2,1)}, bf16[256,1280]{1,0:T(8,128)(2,1)}, bf16[256,1280]{1,0:T(8,128)(2,1)}) custom-call(bf16[4,256,1280]{2,1,0:T(8,128)(2,1)S(1)} %shard_map.84.packed), custom_call_target="tpu_custom_call" | custom-call | tf_op jit(solution)/shard_map/pallas_call | solution.py:305
